TPU v7x, 256 devices: a whole 4x4x8 slice. The times are simulated.
256 devices in a mesh: claim: 64 (over y_hi, x, z), feat: 4 (over y_lo, core).
Axes of the slice: x: 4, y: 4 (y_hi: 2, y_lo: 2; y = y_hi * 2 + y_lo), z: 8, core: 2. Of those that a mesh axis runs over, the one named last changes fastest.
Arguments:
- block_tiles: bfloat16 [64, 4, 128, 128, 128], P('claim', 'feat'), may hold values from 0.049804688 to 1
- block_scale: float32 [64, 4, 128], P('claim', 'feat'), may hold values from 1 to 12, as said below
- row_index: int32 [64, 4, 128], P('claim', 'feat'), may hold values from 0 to 63
- col_index: int32 [64, 4, 128], P('claim', 'feat'), may hold values from 0 to 31
- start_basis: float32 [16384, 64], P('feat'), may hold values from -6 to 6
Outputs:
- claim_basis: float32 [524288, 64], P(('claim', 'feat'))
- feature_basis: float32 [16384, 64], P(('feat', 'claim'))
- bidiagonal: float32 [4, 64, 64], replicated
Inputs may be any that keep to these rules, and one draw needn't show every extreme that they name: `row_index`: row block within the device's 64 row blocks of claims; a few row blocks hold most stored blocks. `col_index`: column block within the device's 32 column blocks. `block_scale`: positive block scales.
All inputs are finite; a program needn't handle non-finite values.
Results may differ from a plain program's by a relative error of at most 0.012.
Values may be sent and summed in bfloat16 or wider, within the bound.
A program may use at most 64 MiB of HBM per device.

v0:
```python
import jax
import jax.numpy as jnp
from jax import lax
from jax.sharding import PartitionSpec as P

BLK_ROWS = 64
HIGH = lax.Precision.HIGHEST


def forward_local(block_tiles, block_scale, row_index, col_index, operand):
    edge = block_tiles.shape[-1]
    width = operand.shape[-1]
    picked = operand.reshape(-1, edge, width)[col_index]
    products = jnp.einsum("bij,bjk->bik", block_tiles, picked, preferred_element_type=jnp.float32)
    products = products * block_scale[:, None, None]
    selector = (row_index[None, :] == jnp.arange(BLK_ROWS, dtype=jnp.int32)[:, None]).astype(
        jnp.float32
    )
    summed = jnp.einsum("rb,bik->rik", selector, products, precision=HIGH)
    return summed.reshape(BLK_ROWS * edge, width)


def backward_local(block_tiles, block_scale, row_index, col_index, operand, col_count):
    edge = block_tiles.shape[-1]
    width = operand.shape[-1]
    picked = operand.reshape(-1, edge, width)[row_index]
    products = jnp.einsum("bij,bik->bjk", block_tiles, picked, preferred_element_type=jnp.float32)
    products = products * block_scale[:, None, None]
    selector = (col_index[None, :] == jnp.arange(col_count, dtype=jnp.int32)[:, None]).astype(
        jnp.float32
    )
    summed = jnp.einsum("cb,bjk->cjk", selector, products, precision=HIGH)
    return summed.reshape(col_count * edge, width)


def degree_local(block_tiles, block_scale, row_index, col_index, col_count):
    row_sums = jnp.sum(block_tiles, axis=2, dtype=jnp.float32) * block_scale[:, None]
    col_sums = jnp.sum(block_tiles, axis=1, dtype=jnp.float32) * block_scale[:, None]
    row_select = (row_index[None, :] == jnp.arange(BLK_ROWS, dtype=jnp.int32)[:, None]).astype(
        jnp.float32
    )
    col_select = (col_index[None, :] == jnp.arange(col_count, dtype=jnp.int32)[:, None]).astype(
        jnp.float32
    )
    row_part = jnp.einsum("rb,bi->ri", row_select, row_sums, precision=HIGH).reshape(-1)
    col_part = jnp.einsum("cb,bi->ci", col_select, col_sums, precision=HIGH).reshape(-1)
    return (row_part, col_part)


def gram_of(block):
    return jnp.dot(block.T, block, precision=HIGH)


def orthonormal(block, gram_total):
    factor = jnp.linalg.cholesky(gram_total)
    basis = lax.linalg.triangular_solve(
        factor, block, left_side=False, lower=True, transpose_a=True
    )
    return (basis, factor.T)


def per_device(block_tiles, block_scale, row_index, col_index, start_basis):
    tiles_here = block_tiles.reshape(block_tiles.shape[2:])
    scale_here = block_scale.reshape(-1)
    rows_here = row_index.reshape(-1)
    cols_here = col_index.reshape(-1)
    edge = tiles_here.shape[-1]
    col_count = start_basis.shape[0] // edge
    claim_count = lax.axis_size("claim")
    own_cols = start_basis.shape[0] // claim_count
    own_first = lax.axis_index("claim") * own_cols
    row_part, col_part = degree_local(tiles_here, scale_here, rows_here, cols_here, col_count)
    col_total = lax.psum(col_part, "claim")
    col_scale = lax.rsqrt(col_total + 1.0)
    row_total = lax.psum_scatter(row_part, "feat", scatter_dimension=0, tiled=True)
    start_total = lax.psum(gram_of(start_basis), "feat")
    first_basis, _ = orthonormal(start_basis, start_total)
    first_operand = (col_scale[:, None] * first_basis).astype(jnp.bfloat16)
    first_partial = forward_local(tiles_here, scale_here, rows_here, cols_here, first_operand)
    first_sums = lax.psum_scatter(first_partial, "feat", scatter_dimension=0, tiled=True)
    row_scale = lax.rsqrt(row_total + 1.0)

    def row_orthonormal(block):
        total = lax.psum(gram_of(block), ("claim", "feat"))
        return orthonormal(block, total)

    def backward_partial(basis):
        operand = (row_scale[:, None] * basis).astype(jnp.bfloat16)
        gathered = lax.all_gather(operand, "feat", axis=0, tiled=True)
        return backward_local(tiles_here, scale_here, rows_here, cols_here, gathered, col_count)

    def column_update(partial_value, previous, coupling):
        summed = lax.psum(partial_value, "claim")
        update = col_scale[:, None] * summed - jnp.dot(previous, coupling.T, precision=HIGH)
        total = lax.psum(gram_of(update), "feat")
        return orthonormal(update, total)

    u_first, b_first = row_orthonormal(row_scale[:, None] * first_sums)
    v_second, a_second = column_update(backward_partial(u_first), first_basis, b_first)
    scaled = (col_scale[:, None] * v_second).astype(jnp.bfloat16)
    second_partial = forward_local(tiles_here, scale_here, rows_here, cols_here, scaled)
    second_sums = lax.psum_scatter(second_partial, "feat", scatter_dimension=0, tiled=True)
    p_second = row_scale[:, None] * second_sums - jnp.dot(u_first, a_second.T, precision=HIGH)
    u_second, b_second = row_orthonormal(p_second)
    v_third, a_third = column_update(backward_partial(u_second), v_second, b_second)
    v_output = lax.dynamic_slice_in_dim(v_third, own_first, own_cols, 0)
    bidiagonal = jnp.stack([b_first, a_second, b_second, a_third])
    return (u_second, v_output, bidiagonal)


def solution(mesh):
    placed = (
        P("claim", "feat", None, None, None),
        P("claim", "feat", None),
        P("claim", "feat", None),
        P("claim", "feat", None),
        P("feat", None),
    )
    return jax.shard_map(
        per_device,
        mesh=mesh,
        in_specs=placed,
        out_specs=(P(("claim", "feat"), None), P(("feat", "claim"), None), P()),
        check_vma=False,
    )
```

profile of v0, /device:TPU:1, one launch (start us, length us, event | category | flops | bytes accessed | tf_op | source)
XLA Modules:
  0.0 2190.3 jit_solution(12832989908346976326)
XLA Ops:
  7.3 1.1 copy-done
  9.4 3.4 convert_reduce_fusion.1
  13.1 13.1 all-reduce.1
  26.3 5.8 cholesky.89
  33.5 4.9 custom-call.11
  39.6 305.2 %psum.56 = f32[4096]{0:T(1024)S(1)} all-reduce(f32[4096]{0:T(1024)S(1)} %convolution_bitcast_fusion.6), channel_id=1, replica_groups=mesh['claim'=64,'feat'=4] {'claim'}, use_global_device_ids=true, to_apply=%region_3.0 | all-reduce | flops 4096 | bytes 32768 | tf_op jit(solution)/shard_map/psum | solution.py:73
  345.0 2.2 gather_fusion
  347.1 5.8 multiply_bitcast_fusion.3
  352.9 4.2 fusion.14
  357.1 2.5 copy.86
  361.0 77.3 %reduce-scatter.3.cloned.1.call-done = f32[2048,64]{0,1:T(8,128)} async-done(((f32[8192,64]{0,1:T(8,128)}), f32[2048,64]{0,1:T(8,128)}) %reduce-scatter.3.cloned.1.call-update) | async-done | bytes 524304 | tf_op jit(solution)/shard_map/reduce_scatter | solution.py:80
  438.3 1.8 fusion.27
  440.1 77.1 %psum.58 = f32[64,64]{0,1:T(8,128)S(1)} all-reduce(f32[64,64]{0,1:T(8,128)S(1)} %fusion.27), channel_id=1, replica_groups=mesh['claim'=64,'feat'=4] {'claim','feat'}, use_global_device_ids=true, to_apply=%region_8.11 | all-reduce | flops 4096 | bytes 32768 | tf_op jit(solution)/shard_map/psum | solution.py:84
  517.4 5.8 cholesky.100
  524.5 4.9 custom-call.12
  529.4 2.6 multiply_convert_fusion.3
  532.3 19.8 all-gather.3.cloned.1.call-done
  552.1 1.5 copy_bitcast_fusion.5
  553.6 2.2 gather_fusion.1
  555.8 4.0 multiply_bitcast_fusion.2
  559.8 3.9 fusion.12
  563.8 1.6 copy.88
  565.5 648.9 %all-reduce.5.cloned.1.call-done = f32[4096,64]{0,1:T(8,128)} async-done(((f32[4096,64]{0,1:T(8,128)}), f32[4096,64]{0,1:T(8,128)}) %all-reduce.5.cloned.1.call-update) | async-done | bytes 1048592 | tf_op jit(solution)/shard_map/psum | solution.py:93
  1214.4 2.9 convolution_subtract_fusion.1
  1218.3 56.8 %psum.60 = f32[64,64]{0,1:T(8,128)S(1)} all-reduce(f32[64,64]{0,1:T(8,128)S(1)} %fusion.97), channel_id=1, replica_groups=mesh['claim'=64,'feat'=4] {'feat'}, use_global_device_ids=true, to_apply=%region_10.14 | all-reduce | flops 4096 | bytes 32768 | tf_op jit(solution)/shard_map/psum | solution.py:95
  1275.2 5.8 cholesky.111
  1282.4 4.9 custom-call.13
  1288.5 2.2 gather_fusion.2
  1290.7 5.8 multiply_bitcast_fusion.1
  1296.5 4.2 fusion.10
  1300.6 2.5 copy.85
  1303.2 28.4 %reduce-scatter.5.cloned.1.call-done = f32[2048,64]{0,1:T(8,128)} async-done(((f32[8192,64]{0,1:T(8,128)}), f32[2048,64]{0,1:T(8,128)}) %reduce-scatter.5.cloned.1.call-update) | async-done | bytes 524304 | tf_op jit(solution)/shard_map/reduce_scatter | solution.py:102
  1331.6 2.3 convolution_subtract_fusion.2
  1334.5 77.3 %psum.61 = f32[64,64]{0,1:T(8,128)S(1)} all-reduce(f32[64,64]{0,1:T(8,128)S(1)} %fusion.98), channel_id=1, replica_groups=mesh['claim'=64,'feat'=4] {'claim','feat'}, use_global_device_ids=true, to_apply=%region_12.16 | all-reduce | flops 4096 | bytes 32768 | tf_op jit(solution)/shard_map/psum | solution.py:84
  1411.9 5.8 cholesky.122
  1419.1 4.9 custom-call.14
  1424.0 1.5 multiply_convert_fusion.2
  1425.6 20.0 all-gather.5.cloned.1.call-done
  1445.6 1.5 copy_bitcast_fusion.4
  1447.2 2.2 gather_fusion.3
  1449.3 4.0 multiply_bitcast_fusion
  1453.4 3.9 fusion.8
  1457.3 1.6 copy.87
  1459.0 648.9 %all-reduce.7.cloned.1.call-done = f32[4096,64]{0,1:T(8,128)} async-done(((f32[4096,64]{0,1:T(8,128)}), f32[4096,64]{0,1:T(8,128)}) %all-reduce.7.cloned.1.call-update) | async-done | bytes 1048592 | tf_op jit(solution)/shard_map/psum | solution.py:93
  2107.9 2.9 convolution_subtract_fusion
  2111.8 56.6 %psum.63 = f32[64,64]{0,1:T(8,128)S(1)} all-reduce(f32[64,64]{0,1:T(8,128)S(1)} %fusion.99), channel_id=1, replica_groups=mesh['claim'=64,'feat'=4] {'feat'}, use_global_device_ids=true, to_apply=%region_14.18 | all-reduce | flops 4096 | bytes 32768 | tf_op jit(solution)/shard_map/psum | solution.py:95
  2168.5 5.8 cholesky.133
  2175.7 4.9 custom-call.15
  (70 shorter events, 17.1 us)
Async XLA Ops:
  7.2 1.2 copy-start
  7.2 5.6 copy-start.2
  7.2 5.6 copy-start.3
  7.2 32.2 %copy-start.4 = (s32[1,1,128]{2,1,0:T(1,128)S(1)}, s32[1,1,128]{2,1,0:T(1,128)}, u32[]{:S(2)}) copy-start(s32[1,1,128]{2,1,0:T(1,128)} %param.13) | copy-start | bytes 1540
  7.2 431.1 %reduce-scatter.3.cloned.1.call-start = ((), (), s32[]{:S(2)}) async-start(), calls=%async_computation.2 | async-start | bytes 2621440 | tf_op jit(solution)/shard_map/reduce_scatter | solution.py:80
  357.1 2.6 copy-start.5
  359.7 192.4 %all-gather.3.cloned.1.call-start = ((), (), s32[]{:S(2)}) async-start(), calls=%async_computation.3 | async-start | bytes 1310720 | tf_op jit(solution)/shard_map/all_gather | solution.py:89
  532.0 682.4 %all-reduce.5.cloned.1.call-start = ((), (), s32[]{:S(2)}) async-start(), calls=%async_computation.4 | async-start | bytes 2097152 | tf_op jit(solution)/shard_map/psum | solution.py:93
  565.4 766.2 %reduce-scatter.5.cloned.1.call-start = ((), (), s32[]{:S(2)}) async-start(), calls=%async_computation.5 | async-start | bytes 2621440 | tf_op jit(solution)/shard_map/reduce_scatter | solution.py:102
  1300.6 31.0 %copy-start.1 = (f32[2048,64]{0,1:T(8,128)S(1)}, f32[2048,64]{0,1:T(8,128)}, u32[]{:S(2)}) copy-start(f32[2048,64]{0,1:T(8,128)} %get-tuple-element.28) | copy-start | bytes 1572868
  1303.2 142.4 %all-gather.5.cloned.1.call-start = ((), (), s32[]{:S(2)}) async-start(), calls=%async_computation.6 | async-start | bytes 1310720 | tf_op jit(solution)/shard_map/all_gather | solution.py:89
  1425.6 682.3 %all-reduce.7.cloned.1.call-start = ((), (), s32[]{:S(2)}) async-start(), calls=%async_computation.7 | async-start | bytes 2097152 | tf_op jit(solution)/shard_map/psum | solution.py:93
Sparse Core Ops, SparseCore 0:
  359.8 78.4 reduce-scatter.2
  532.2 19.9 all-gather.2
  565.6 648.7 all-reduce.4
  1303.3 28.2 reduce-scatter.4
  1425.7 19.9 all-gather.4
  1459.1 648.7 all-reduce.6
where the time goes:
time: 2200 us; the launch traced here: 2190 us
  waiting for transfers between devices  1440 us (65%)
  blocking collectives  586 us (27%)
  other arithmetic  64.1 us (3%)
  matrix products  57 us (3%)
  local copies, waits for them, and re-layouts  23.7 us (1%)
    psum x2, waiting for transfers between devices, column_update(): summed = lax.psum(partial_value, 'claim')  1300 us
    psum x1, blocking collectives, per_device(): col_total = lax.psum(col_part, 'claim')  305 us
    psum x2, blocking collectives, row_orthonormal(): total = lax.psum(gram_of(block), ('claim', 'feat'))  154 us
    psum x2, blocking collectives, column_update(): total = lax.psum(gram_of(update), 'feat')  113 us
    reduce_scatter x1, waiting for transfers between devices, per_device(): lax.psum_scatter(first_partial, 'feat', scatter_dimension=0, tiled=True)  77.3 us
  transfers between devices with their start and end apart: 6, of which 6 were waited for; matrix products, arithmetic and copies ran while one was open for 0% of the time, Pallas kernels for 0%

commit v1 on v0

--- a/solution.py
+++ b/solution.py
@@ -81,7 +81,9 @@
     row_scale = lax.rsqrt(row_total + 1.0)
 
     def row_orthonormal(block):
-        total = lax.psum(gram_of(block), ("claim", "feat"))
+        total = gram_of(block)
+        for mesh_axis in ("claim", "feat"):
+            total = lax.psum(total, mesh_axis)
         return orthonormal(block, total)
 
     def backward_partial(basis):

time: 2200 us -> 2770 us (1.26)
  blocking collectives: 586 us -> 1170 us
    psum x2 -> x4, blocking collectives: 154 us -> 737 us  [row_orthonormal(): total = lax.psum(total, mesh_axis)]
where the time goes in v1:
time: 2770 us; the launch traced here: 2760 us
  waiting for transfers between devices  1430 us (52%)
  blocking collectives  1170 us (42%)
  other arithmetic  64.1 us (2%)
  matrix products  57 us (2%)
    psum x2, waiting for transfers between devices, column_update(): summed = lax.psum(partial_value, 'claim')  1300 us
    psum x4, blocking collectives, row_orthonormal(): total = lax.psum(total, mesh_axis)  737 us
    psum x1, blocking collectives, per_device(): col_total = lax.psum(col_part, 'claim')  305 us
    psum x2, blocking collectives, column_update(): total = lax.psum(gram_of(update), 'feat')  113 us
    reduce_scatter x1, waiting for transfers between devices, per_device(): lax.psum_scatter(first_partial, 'feat', scatter_dimension=0, tiled=True)  77.3 us
  transfers between devices with their start and end apart: 6, of which 6 were waited for; matrix products, arithmetic and copies ran while one was open for 0% of the time, Pallas kernels for 0%

profile of v1, /device:TPU:1, one launch (start us, length us, event | category | flops | bytes accessed | tf_op | source)
XLA Modules:
  0.0 2763.5 jit_solution(7869802394764516723)
XLA Ops:
  9.4 3.4 convert_reduce_fusion.1
  13.1 13.1 all-reduce.1
  26.3 5.8 cholesky.89
  33.5 4.9 custom-call.11
  39.6 305.2 %psum.70 = f32[4096]{0:T(1024)S(1)} all-reduce(f32[4096]{0:T(1024)S(1)} %convolution_bitcast_fusion.6), channel_id=1, replica_groups=mesh['claim'=64,'feat'=4] {'claim'}, use_global_device_ids=true, to_apply=%region_3.0 | all-reduce | flops 4096 | bytes 32768 | tf_op jit(solution)/shard_map/psum | solution.py:73
  345.0 2.2 gather_fusion
  347.1 5.8 multiply_bitcast_fusion.3
  352.9 4.2 fusion.14
  357.1 2.5 copy.86
  361.0 77.3 %reduce-scatter.3.cloned.1.call-done = f32[2048,64]{0,1:T(8,128)} async-done(((f32[8192,64]{0,1:T(8,128)}), f32[2048,64]{0,1:T(8,128)}) %reduce-scatter.3.cloned.1.call-update) | async-done | bytes 524304 | tf_op jit(solution)/shard_map/reduce_scatter | solution.py:80
  438.3 1.8 fusion.27
  440.1 303.0 %psum.72 = f32[64,64]{0,1:T(8,128)S(1)} all-reduce(f32[64,64]{0,1:T(8,128)S(1)} %fusion.27), channel_id=1, replica_groups=mesh['claim'=64,'feat'=4] {'claim'}, use_global_device_ids=true, to_apply=%region_8.11 | all-reduce | flops 4096 | bytes 32768 | tf_op jit(solution)/shard_map/psum | solution.py:86
  743.1 65.3 %psum.73 = f32[64,64]{0,1:T(8,128)S(1)} all-reduce(f32[64,64]{0,1:T(8,128)S(1)} %psum.72), channel_id=1, replica_groups=mesh['claim'=64,'feat'=4] {'feat'}, use_global_device_ids=true, to_apply=%region_9.12 | all-reduce | flops 4096 | bytes 32768 | tf_op jit(solution)/shard_map/psum | solution.py:86
  808.5 5.8 cholesky.100
  815.7 4.9 custom-call.12
  820.6 2.6 multiply_convert_fusion.3
  823.5 15.2 all-gather.3.cloned.1.call-done
  838.7 1.5 copy_bitcast_fusion.5
  840.2 2.2 gather_fusion.1
  842.4 4.0 multiply_bitcast_fusion.2
  846.5 3.9 fusion.12
  850.4 1.6 copy.88
  852.1 648.9 %all-reduce.5.cloned.1.call-done = f32[4096,64]{0,1:T(8,128)} async-done(((f32[4096,64]{0,1:T(8,128)}), f32[4096,64]{0,1:T(8,128)}) %all-reduce.5.cloned.1.call-update) | async-done | bytes 1048592 | tf_op jit(solution)/shard_map/psum | solution.py:95
  1501.0 2.9 convolution_subtract_fusion.1
  1504.9 56.8 %psum.75 = f32[64,64]{0,1:T(8,128)S(1)} all-reduce(f32[64,64]{0,1:T(8,128)S(1)} %fusion.97), channel_id=1, replica_groups=mesh['claim'=64,'feat'=4] {'feat'}, use_global_device_ids=true, to_apply=%region_11.15 | all-reduce | flops 4096 | bytes 32768 | tf_op jit(solution)/shard_map/psum | solution.py:97
  1561.8 5.8 cholesky.111
  1569.0 4.9 custom-call.13
  1575.1 2.2 gather_fusion.2
  1577.3 5.8 multiply_bitcast_fusion.1
  1583.1 4.2 fusion.10
  1587.2 2.5 copy.85
  1589.9 28.4 %reduce-scatter.5.cloned.1.call-done = f32[2048,64]{0,1:T(8,128)} async-done(((f32[8192,64]{0,1:T(8,128)}), f32[2048,64]{0,1:T(8,128)}) %reduce-scatter.5.cloned.1.call-update) | async-done | bytes 524304 | tf_op jit(solution)/shard_map/reduce_scatter | solution.py:104
  1618.3 2.3 convolution_subtract_fusion.2
  1621.1 303.0 %psum.76 = f32[64,64]{0,1:T(8,128)S(1)} all-reduce(f32[64,64]{0,1:T(8,128)S(1)} %fusion.98), channel_id=1, replica_groups=mesh['claim'=64,'feat'=4] {'claim'}, use_global_device_ids=true, to_apply=%region_13.17 | all-reduce | flops 4096 | bytes 32768 | tf_op jit(solution)/shard_map/psum | solution.py:86
  1924.1 65.6 %psum.77 = f32[64,64]{0,1:T(8,128)S(1)} all-reduce(f32[64,64]{0,1:T(8,128)S(1)} %psum.76), channel_id=1, replica_groups=mesh['claim'=64,'feat'=4] {'feat'}, use_global_device_ids=true, to_apply=%region_14.18 | all-reduce | flops 4096 | bytes 32768 | tf_op jit(solution)/shard_map/psum | solution.py:86
  1989.8 5.8 cholesky.122
  1997.0 4.9 custom-call.14
  2001.9 1.5 multiply_convert_fusion.2
  2003.5 15.4 all-gather.5.cloned.1.call-done
  2020.4 2.2 gather_fusion.3
  2022.5 4.0 multiply_bitcast_fusion
  2026.6 3.9 fusion.8
  2030.5 1.6 copy.87
  2032.2 648.9 %all-reduce.7.cloned.1.call-done = f32[4096,64]{0,1:T(8,128)} async-done(((f32[4096,64]{0,1:T(8,128)}), f32[4096,64]{0,1:T(8,128)}) %all-reduce.7.cloned.1.call-update) | async-done | bytes 1048592 | tf_op jit(solution)/shard_map/psum | solution.py:95
  2681.1 2.9 convolution_subtract_fusion
  2685.0 56.6 %psum.79 = f32[64,64]{0,1:T(8,128)S(1)} all-reduce(f32[64,64]{0,1:T(8,128)S(1)} %fusion.99), channel_id=1, replica_groups=mesh['claim'=64,'feat'=4] {'feat'}, use_global_device_ids=true, to_apply=%region_16.20 | all-reduce | flops 4096 | bytes 32768 | tf_op jit(solution)/shard_map/psum | solution.py:97
  2741.7 5.8 cholesky.133
  2748.9 4.9 custom-call.15
  (72 shorter events, 19.8 us)
Async XLA Ops:
  7.2 1.2 copy-start
  7.2 5.6 copy-start.2
  7.2 5.6 copy-start.3
  7.2 32.2 %copy-start.4 = (s32[1,1,128]{2,1,0:T(1,128)S(1)}, s32[1,1,128]{2,1,0:T(1,128)}, u32[]{:S(2)}) copy-start(s32[1,1,128]{2,1,0:T(1,128)} %param.13) | copy-start | bytes 1540
  7.2 431.1 %reduce-scatter.3.cloned.1.call-start = ((), (), s32[]{:S(2)}) async-start(), calls=%async_computation.2 | async-start | bytes 2621440 | tf_op jit(solution)/shard_map/reduce_scatter | solution.py:80
  357.1 2.6 copy-start.5
  359.7 479.0 %all-gather.3.cloned.1.call-start = ((), (), s32[]{:S(2)}) async-start(), calls=%async_computation.3 | async-start | bytes 1310720 | tf_op jit(solution)/shard_map/all_gather | solution.py:91
  823.2 677.8 %all-reduce.5.cloned.1.call-start = ((), (), s32[]{:S(2)}) async-start(), calls=%async_computation.4 | async-start | bytes 2097152 | tf_op jit(solution)/shard_map/psum | solution.py:95
  852.1 766.2 %reduce-scatter.5.cloned.1.call-start = ((), (), s32[]{:S(2)}) async-start(), calls=%async_computation.5 | async-start | bytes 2621440 | tf_op jit(solution)/shard_map/reduce_scatter | solution.py:104
  1587.2 31.0 %copy-start.1 = (f32[2048,64]{0,1:T(8,128)S(1)}, f32[2048,64]{0,1:T(8,128)}, u32[]{:S(2)}) copy-start(f32[2048,64]{0,1:T(8,128)} %get-tuple-element.28) | copy-start | bytes 1572868
  1589.8 429.0 %all-gather.5.cloned.1.call-start = ((), (), s32[]{:S(2)}) async-start(), calls=%async_computation.6 | async-start | bytes 1310720 | tf_op jit(solution)/shard_map/all_gather | solution.py:91
  2003.4 677.7 %all-reduce.7.cloned.1.call-start = ((), (), s32[]{:S(2)}) async-start(), calls=%async_computation.7 | async-start | bytes 2097152 | tf_op jit(solution)/shard_map/psum | solution.py:95
Sparse Core Ops, SparseCore 0:
  359.8 78.4 reduce-scatter.2
  823.3 15.3 all-gather.2
  852.2 648.7 all-reduce.4
  1589.9 28.2 reduce-scatter.4
  2003.6 15.2 all-gather.4
  2032.3 648.7 all-reduce.6
